TPU v7x, 256 devices: a whole 4x4x8 slice. The times are simulated.
256 devices in a mesh: rows: 32 (over z_hi, y, core), rep: 8 (over z_lo, x).
Axes of the slice: x: 4, y: 4, z: 8 (z_hi: 4, z_lo: 2; z = z_hi * 2 + z_lo), core: 2. Of those that a mesh axis runs over, the one named last changes fastest.
Arguments:
- features: bfloat16 [32768, 256], P('rows'), may hold values from -6 to 6
- inv_sqrt_degree: bfloat16 [32768], P('rows'), may hold values from 0.25 to 1
- weight: bfloat16 [256, 256], replicated, may hold values from -0.375 to 0.375
- tile_vals: bfloat16 [32, 1024, 128, 128], P('rows', 'rep'), may hold values from -0.046875 to 0.046875
- tile_row: int32 [32, 1024], P('rows', 'rep'), may hold values from 0 to 7, as said below
- tile_col: int32 [32, 1024], P('rows', 'rep'), may hold values from 0 to 31, as said below
- tile_count: int32 [32, 32], P('rows', 'rep'), may hold values from 0 to 64, as said below
- cotangent: bfloat16 [32768, 256], P('rows'), may hold values from -6 to 6
Outputs:
- activated: bfloat16 [32768, 256], P(('rows', 'rep'))
- weight_grad: float32 [256, 256], replicated
- feature_grad: bfloat16 [32768, 256], P(('rep', 'rows'))
Inputs may be any that keep to these rules, and one draw needn't show every extreme that they name: `tile_count`: each count is at most 64; the 4 counts of row block i and columns r * 4 .. r * 4 + 3 sum to at most 128. Some pair holds exactly 64 tiles and some block row and replica exactly 128, in every draw. `tile_row`: the valid slots of a block row and replica are ordered by column block, and inside one block pair their positions are distinct. A valid slot counted for column block r * 4 + s has tile_col between s * 8 and s * 8 + 7.
All inputs are finite; a program needn't handle non-finite values.
Results may differ from a plain program's by a relative error of at most 0.015.
Values may be sent and summed in bfloat16 or wider, within the bound.
No kernel may reach another device: no remote copies, remote signals or barrier semaphores. Data moves between devices by JAX's collectives and lax.ppermute only.
A program may use at most 128 MiB of HBM per device.

v0:
```python
import jax
import jax.numpy as jnp
from jax import lax
from jax.sharding import PartitionSpec as P


def from_root(shard, axis, root):
    mine = lax.axis_index(axis) == root
    return lax.psum(jnp.where(mine, shard, jnp.zeros_like(shard)), axis)


def tile_products(values, out_index, in_index, keep, source, out_tiles, flipped):
    count = values.shape[0]
    block_size = 32
    turns = count // block_size
    width = source.shape[-1]
    tile = values.shape[-1]

    def advance(carry, block):
        vals_block, out_block, in_block, keep_block = block
        picked = source[in_block]
        if flipped:
            prod = jnp.einsum(
                "kji,kjf->kif", vals_block, picked, preferred_element_type=jnp.float32
            )
        else:
            prod = jnp.einsum(
                "kij,kjf->kif", vals_block, picked, preferred_element_type=jnp.float32
            )
        prod = jnp.where(keep_block[:, None, None], prod, jnp.float32(0.0))
        return (carry.at[out_block].add(prod), None)

    blocks = (
        values.reshape(turns, block_size, tile, tile),
        out_index.reshape(turns, block_size),
        in_index.reshape(turns, block_size),
        keep.reshape(turns, block_size),
    )
    initial = jnp.zeros((out_tiles, tile, width), jnp.float32)
    result, _ = lax.scan(advance, initial, blocks)
    return result


def section_window(values, out_rows, in_cols, starts, ends, section, per_block):
    slots = values.shape[0]
    pair_slots = per_block * per_block
    first = jnp.clip(starts[section], 0, slots - pair_slots)
    index = first + jnp.arange(pair_slots, dtype=jnp.int32)
    keep = (index >= starts[section]) & (index < ends[section])
    vals_window = lax.dynamic_slice_in_dim(values, first, pair_slots, 0)
    rows_window = lax.dynamic_slice_in_dim(out_rows, first, pair_slots, 0)
    cols_window = lax.dynamic_slice_in_dim(in_cols, first, pair_slots, 0)
    cols_window = jnp.clip(cols_window - section * per_block, 0, per_block - 1)
    return (vals_window, rows_window, cols_window, keep)


def shards(features, inv_sqrt_degree, weight, tile_vals, tile_row, tile_col, tile_count, cotangent):
    rows_count = lax.axis_size("rows")
    rep_count = lax.axis_size("rep")
    sections = rows_count // rep_count
    replica = lax.axis_index("rep")
    block_row = lax.axis_index("rows")
    nodes_block, width = features.shape
    tile = tile_vals.shape[-1]
    per_block = nodes_block // tile
    share = nodes_block // rep_count
    values = tile_vals[0]
    out_rows = tile_row[0]
    in_cols = tile_col[0]
    counts = tile_count[0]
    degree = inv_sqrt_degree.astype(jnp.float32)[:, None]
    scaled = (degree * features.astype(jnp.float32)).astype(jnp.bfloat16)
    ends = jnp.cumsum(counts)
    starts = ends - counts
    grad_factor = float(nodes_block * rows_count) ** (-0.5)
    arrived = []
    forward_sum = jnp.zeros((per_block, tile, width), jnp.float32)
    for section in range(sections):
        root = replica * sections + section
        block_feats, block_degree = (
            from_root(scaled, "rows", root),
            from_root(inv_sqrt_degree, "rows", root),
        )
        arrived.append((block_feats, block_degree))
        vals_window, rows_window, cols_window, keep = section_window(
            values, out_rows, in_cols, starts, ends, section, per_block
        )
        source = block_feats.reshape(per_block, tile, width)
        forward_sum = forward_sum + tile_products(
            vals_window, rows_window, cols_window, keep, source, per_block, False
        )
    partial_rows = forward_sum.reshape(nodes_block, width)
    summed = lax.psum(partial_rows, "rep")
    propagated = (degree * (summed + scaled.astype(jnp.float32))).astype(jnp.bfloat16)
    preact = jnp.dot(propagated, weight, preferred_element_type=jnp.float32)
    gate = jax.nn.sigmoid(preact)
    activated_block = (preact * gate).astype(jnp.bfloat16)
    grad_pre = (cotangent.astype(jnp.float32) * gate * (1.0 + preact * (1.0 - gate))).astype(
        jnp.bfloat16
    )
    back = (degree * jnp.dot(grad_pre, weight.T, preferred_element_type=jnp.float32)).astype(
        jnp.bfloat16
    )
    activated = lax.dynamic_slice_in_dim(activated_block, replica * share, share, 0)
    prop_share = lax.dynamic_slice_in_dim(propagated, replica * share, share, 0)
    grad_share = lax.dynamic_slice_in_dim(grad_pre, replica * share, share, 0)
    local_grad = lax.dot_general(
        prop_share, grad_share, (((0,), (0,)), ((), ())), preferred_element_type=jnp.float32
    )
    weight_grad = lax.psum(local_grad * grad_factor, ("rows", "rep"))
    back_tiles = back.reshape(per_block, tile, width)
    pieces = []
    for section in range(sections):
        vals_window, rows_window, cols_window, keep = section_window(
            values, out_rows, in_cols, starts, ends, section, per_block
        )
        pieces.append(
            tile_products(vals_window, cols_window, rows_window, keep, back_tiles, per_block, True)
        )
    terms = jnp.stack(pieces).reshape(sections, nodes_block, width)
    own_section = block_row - replica * sections
    section_ids = jnp.arange(sections, dtype=jnp.int32)
    self_part = jnp.where(
        (section_ids == own_section)[:, None, None],
        back.astype(jnp.float32)[None, :, :],
        jnp.float32(0.0),
    )
    degrees = jnp.stack([pair[1] for pair in arrived]).astype(jnp.float32)
    terms = (terms + self_part) * degrees[:, :, None]
    feature_grad = lax.psum_scatter(
        terms.reshape(sections * nodes_block, width), "rows", scatter_dimension=0, tiled=True
    ).astype(jnp.bfloat16)
    return (activated, weight_grad, feature_grad)


def solution(mesh):
    placed = (
        P("rows", None),
        P("rows"),
        P(),
        P("rows", "rep", None, None),
        P("rows", "rep"),
        P("rows", "rep"),
        P("rows", "rep"),
        P("rows", None),
    )
    return jax.shard_map(
        shards,
        mesh=mesh,
        in_specs=placed,
        out_specs=(P(("rows", "rep"), None), P(), P(("rep", "rows"), None)),
        check_vma=False,
    )
```

profile of v0, /device:TPU:2, one launch (start us, length us, event | category | flops | bytes accessed | tf_op | source)
XLA Modules:
  0.0 1060.3 jit_solution(3447704333140686903)
XLA Ops:
  20.7 9.3 constant_dynamic-slice_fusion.23
  30.0 276.2 %all-reduce.10.cloned.1.call-done = (bf16[8,128,256]{2,1,0:T(8,128)(2,1)}, bf16[8,128,256]{2,1,0:T(8,128)(2,1)}, bf16[8,128,256]{2,1,0:T(8,128)(2,1)}, bf16[8,128,256]{2,1,0:T(8,128)(2,1)}) async-done(((bf16[8,128,256]{2,1,0:T(8,128)(2,1)}, bf16[8,128,256]{2,1,0:T(8,128)(2,1)}, bf16[8,128,256]{2,1,0:T(8,128)(2,1)}, bf16[8,128,256]{2,1,0:T(8,128)(2,1)}), (bf16[8,128,256]{2,1,0:T(8,128)(2,1)}, ...) | async-done | bytes 2097168 | tf_op jit(solution)/shard_map/psum | solution.py:9
  306.3 28.3 %while.83 = (s32[]{:T(128)}, f32[8,128,256]{2,1,0:T(8,128)S(1)}, s32[2,32]{1,0:T(2,128)S(1)}, pred[2,32]{1,0:T(4,128)(4,1)S(1)}, bf16[2,32,128,128]{3,2,1,0:T(8,...) while((s32[]{:T(128)}, f32[8,128,256]{2,1,0:T(8,128)S(1)}, ...), condition=%wide.region_16.17_spmd, body=%wide.region_14.16_spmd.sunk | while | flops 270533824 | bytes 24122440 | solution.py:40
  314.0 6.5 scatter_fusion.3
  328.2 6.5 scatter_fusion.3
  334.7 26.2 %while.82 = (s32[]{:T(128)}, f32[8,128,256]{2,1,0:T(8,128)S(1)}, s32[2,32]{1,0:T(2,128)S(1)}, pred[2,32]{1,0:T(4,128)(4,1)S(1)}, bf16[2,32,128,128]{3,2,1,0:T(8,...) while((s32[]{:T(128)}, f32[8,128,256]{2,1,0:T(8,128)S(1)}, ...), condition=%wide.region_12.13_spmd, body=%wide.region_10.12_spmd.sunk | while | flops 270533824 | bytes 24122440 | solution.py:40
  341.4 6.5 scatter_fusion.2
  354.5 6.5 scatter_fusion.2
  361.0 28.3 %while.80 = (s32[]{:T(128)}, f32[8,128,256]{2,1,0:T(8,128)S(1)}, s32[2,32]{1,0:T(2,128)S(1)}, pred[2,32]{1,0:T(4,128)(4,1)S(1)}, bf16[2,32,128,128]{3,2,1,0:T(8,...) while((s32[]{:T(128)}, f32[8,128,256]{2,1,0:T(8,128)S(1)}, ...), condition=%wide.region_4.5_spmd, body=%wide.region_2.4_spmd.sunk | while | flops 270533824 | bytes 24122440 | solution.py:40
  368.7 6.5 scatter_fusion
  382.9 6.5 scatter_fusion
  390.4 34.4 %while.81 = (s32[]{:T(128)}, f32[8,128,256]{2,1,0:T(8,128)}, s32[2,32]{1,0:T(2,128)S(1)}, pred[2,32]{1,0:T(4,128)(4,1)S(1)}, bf16[2,32,128,128]{3,2,1,0:T(8,128)...) while((s32[]{:T(128)}, f32[8,128,256]{2,1,0:T(8,128)}, s32[2,32]{1,0:T(2,128)S(1)}, ...), condition=%wide.region_8.9_spmd, body=%wide.region_6.8_spmd.sunk | while | flops 270533824 | bytes 24122440 | solution.py:40
  398.1 9.6 scatter_fusion.1
  415.3 9.5 scatter_fusion.1
  441.7 144.0 %all-reduce = (bf16[1,1024,1]{1,2,0:T(2,128)(2,1)S(1)}, bf16[1,1024,1]{1,2,0:T(2,128)(2,1)S(1)}, bf16[1,1024,1]{1,2,0:T(2,128)(2,1)S(1)}, bf16[1,1024,1]{1,2,0:T(2,128)(2,1)S(1)}) all-reduce(bf16[1,1024,1]{1,2,0:T(2,128)(2,1)S(1)} %stack.41, bf16[1,1024,1]{1,2,0:T(2,128)(2,1)S(1)} %stack.40, ...), channel_id=1, replica_groups=mesh['rows'=32,'rep'=8] {'rows'}, use_global_device_ids=true, to_apply=%region_34.35 | all-reduce | flops 4096 | bytes 16384 | tf_op jit(solution)/shard_map/psum | solution.py:9
  590.5 26.1 %while.87 = (s32[]{:T(128)}, f32[8,128,256]{2,1,0:T(8,128)S(1)}, s32[2,32]{1,0:T(2,128)S(1)}, pred[2,32]{1,0:T(4,128)(4,1)S(1)}, bf16[2,32,128,128]{2,3,1,0:T(8,...) while((s32[]{:T(128)}, f32[8,128,256]{2,1,0:T(8,128)S(1)}, ...), condition=%wide.region_30.31_spmd, body=%wide.region_28.30_spmd.sunk | while | flops 270533824 | bytes 24122440 | solution.py:40
  597.1 6.5 scatter_fusion.7
  610.2 6.4 scatter_fusion.7
  616.8 26.1 %while.86 = (s32[]{:T(128)}, f32[8,128,256]{2,1,0:T(8,128)S(1)}, s32[2,32]{1,0:T(2,128)S(1)}, pred[2,32]{1,0:T(4,128)(4,1)S(1)}, bf16[2,32,128,128]{2,3,1,0:T(8,...) while((s32[]{:T(128)}, f32[8,128,256]{2,1,0:T(8,128)S(1)}, ...), condition=%wide.region_27.28_spmd, body=%wide.region_25.27_spmd.sunk | while | flops 270533824 | bytes 24122440 | solution.py:40
  644.1 28.1 %while.85 = (s32[]{:T(128)}, f32[8,128,256]{2,1,0:T(8,128)}, s32[2,32]{1,0:T(2,128)S(1)}, pred[2,32]{1,0:T(4,128)(4,1)S(1)}, bf16[2,32,128,128]{2,3,1,0:T(8,128)...) while((s32[]{:T(128)}, f32[8,128,256]{2,1,0:T(8,128)}, ...), condition=%wide.region_24.25_spmd, body=%wide.region_22.24_spmd.sunk | while | flops 270533824 | bytes 32511104 | solution.py:40
  672.3 26.1 %while.84 = (s32[]{:T(128)}, f32[8,128,256]{2,1,0:T(8,128)S(1)}, s32[2,32]{1,0:T(2,128)S(1)}, pred[2,32]{1,0:T(4,128)(4,1)S(1)}, bf16[2,32,128,128]{2,3,1,0:T(8,...) while((s32[]{:T(128)}, f32[8,128,256]{2,1,0:T(8,128)S(1)}, ...), condition=%wide.region_21.22_spmd, body=%wide.region_19.21_spmd.sunk | while | flops 270533824 | bytes 24122440 | solution.py:40
  692.0 6.4 scatter_fusion.4
  706.8 91.9 %reduce-scatter.2.cloned.1.call-done = f32[128,256]{1,0:T(8,128)} async-done(((f32[4096,256]{1,0:T(8,128)}), f32[128,256]{1,0:T(8,128)}) %reduce-scatter.2.cloned.1.call-update) | async-done | bytes 131088 | tf_op jit(solution)/shard_map/reduce_scatter | solution.py:130
  800.3 251.8 %all-reduce.8.cloned.1.call-done = f32[256,256]{1,0:T(8,128)} async-done(((f32[256,256]{1,0:T(8,128)}), f32[256,256]{1,0:T(8,128)}) %all-reduce.8.cloned.1.call-update) | async-done | bytes 262160 | tf_op jit(solution)/shard_map/psum | solution.py:110
  (181 shorter events, 192.7 us)
Async XLA Ops:
  7.2 580.1 %copy-start = (bf16[256,256]{1,0:T(8,128)(2,1)S(1)}, bf16[256,256]{1,0:T(8,128)(2,1)}, u32[]{:S(2)}) copy-start(bf16[256,256]{1,0:T(8,128)(2,1)} %param.26) | copy-start | bytes 393220
  7.2 299.0 %all-reduce.10.cloned.1.call-start = ((), (), s32[]{:S(2)}) async-start(), calls=%async_computation.4 | async-start | bytes 4194304 | tf_op jit(solution)/shard_map/psum | solution.py:9
  8.0 2.8 copy-start.16
  8.0 6.2 copy-start.11
  8.0 6.2 copy-start.12
  10.7 575.1 %all-reduce.6.cloned.1.call-start = ((), (), s32[]{:S(2)}) async-start(), calls=%async_computation.1 | async-start | bytes 2097152 | tf_op jit(solution)/shard_map/psum | solution.py:93
  306.3 28.4 %copy-start.5 = (bf16[8,128,256]{2,1,0:T(8,128)(2,1)S(1)}, bf16[8,128,256]{2,1,0:T(8,128)(2,1)}, u32[]{:S(2)}) copy-start(bf16[8,128,256]{2,1,0:T(8,128)(2,1)} %get-tuple-element.943) | copy-start | bytes 1572868
  389.3 1.1 copy-start.13
  427.3 371.4 %reduce-scatter.2.cloned.1.call-start = ((), (), s32[]{:S(2)}) async-start(), calls=%async_computation.3 | async-start | bytes 4325376 | tf_op jit(solution)/shard_map/reduce_scatter | solution.py:130
  427.3 4.2 copy-start.7
  434.5 4.2 copy-start.6
  438.7 147.1 %copy-start.9 = (bf16[1024,256]{1,0:T(8,128)(2,1)S(1)}, bf16[1024,256]{1,0:T(8,128)(2,1)}, u32[]{:S(2)}) copy-start(bf16[1024,256]{1,0:T(8,128)(2,1)} %param.24) | copy-start | bytes 1572868
  441.6 145.7 %copy-start.15 = (bf16[1024,256]{1,0:T(8,128)(2,1)S(1)}, bf16[1024,256]{1,0:T(8,128)(2,1)}, u32[]{:S(2)}) copy-start(bf16[1024,256]{1,0:T(8,128)(2,1)} %param.31) | copy-start | bytes 1572868
  587.3 1.8 copy-start.10
  642.8 1.3 copy-start.2
  644.0 28.3 %copy-start.14 = (pred[2,32]{1,0:T(4,128)(4,1)S(1)}, pred[2,32]{1,0:T(4,128)(4,1)}, u32[]{:S(2)}) copy-start(pred[2,32]{1,0:T(4,128)(4,1)} %copy-done.13) | copy-start | bytes 196
  646.2 4.6 copy-start.3
  657.2 1.0 copy-start.4
  660.2 4.6 copy-start.3
  671.3 1.0 copy-start.4
  698.4 2.0 copy-start.8
  703.3 350.4 %copy-start.1 = (bf16[256,256]{1,0:T(8,128)(2,1)S(1)}, bf16[256,256]{1,0:T(8,128)(2,1)}, u32[]{:S(2)}) copy-start(bf16[256,256]{1,0:T(8,128)(2,1)} %param.26) | copy-start | bytes 393220
  703.4 348.7 %all-reduce.8.cloned.1.call-start = ((), (), s32[]{:S(2)}) async-start(), calls=%async_computation.2 | async-start | bytes 524288 | tf_op jit(solution)/shard_map/psum | solution.py:110
Sparse Core Ops, SparseCore 0:
  10.9 295.2 all-reduce.9
  427.4 79.0 all-reduce.5
  703.5 95.2 reduce-scatter.1
  804.6 247.4 all-reduce.7
where the time goes:
time: 1060 us
  waiting for transfers between devices  620 us (58%)
  blocking collectives  144 us (14%)
  other arithmetic  130 us (12%)
  matrix products  77.7 us (7%)
  local copies, waits for them, and re-layouts  71.1 us (7%)
  between operations  16.7 us (2%)
    psum x1, waiting for transfers between devices, from_root(): return lax.psum(jnp.where(mine, shard, jnp.zeros_like(shard)), axis)  276 us
    psum x1, waiting for transfers between devices, shards(): weight_grad = lax.psum(local_grad * grad_factor, ('rows', 'rep'))  252 us
    psum x1, blocking collectives, from_root(): return lax.psum(jnp.where(mine, shard, jnp.zeros_like(shard)), axis)  144 us
    scatter-add x16, other arithmetic, advance(): return (carry.at[out_block].add(prod), None)  109 us
    reduce_scatter x1, waiting for transfers between devices, shards(): lax.psum_scatter(terms.reshape(sections * nodes_block, width), 'rows', sc...  91.9 us
    gather x16, local copies, waits for them, and re-layouts, advance(): picked = source[in_block]  38.8 us
    dot_general x8, matrix products, advance(): jnp.einsum('kji,kjf->kif', vals_block, picked, preferred_element_type=jnp...  36.5 us
    dot_general x8, matrix products, advance(): jnp.einsum('kij,kjf->kif', vals_block, picked, preferred_element_type=jnp...  36.3 us
  transfers between devices with their start and end apart: 4, of which 3 were waited for; matrix products, arithmetic and copies ran while one was open for 3% of the time, Pallas kernels for 0%

commit v1 on v0

--- a/solution.py
+++ b/solution.py
@@ -6,7 +6,7 @@
 
 def from_root(shard, axis, root):
     mine = lax.axis_index(axis) == root
-    return lax.psum(jnp.where(mine, shard, jnp.zeros_like(shard)), axis)
+    return jnp.sum(lax.all_gather(jnp.where(mine, shard, jnp.zeros_like(shard)), axis), axis=0)
 
 
 def tile_products(values, out_index, in_index, keep, source, out_tiles, flipped):

time: 1060 us -> 1280 us (1.21)
  waiting for transfers between devices: 620 us -> 770 us
  other arithmetic: 130 us -> 176 us
  blocking collectives: 144 us -> 173 us
    all_gather x0 -> x4, waiting for transfers between devices: none -> 421 us  [from_root(): lax.all_gather(jnp.where(mine, shard, jnp.zeros_like(shard)), axis)]
    psum x1 -> x0, waiting for transfers between devices: 276 us -> none  [from_root(): return lax.psum(jnp.where(mine, shard, jnp.zeros_like(shard)), axis)]
    all_gather x0 -> x4, blocking collectives: none -> 173 us  [from_root(): lax.all_gather(jnp.where(mine, shard, jnp.zeros_like(shard)), axis)]
    psum x1 -> x0, blocking collectives: 144 us -> none  [from_root(): return lax.psum(jnp.where(mine, shard, jnp.zeros_like(shard)), axis)]
    reduce_sum x0 -> x8, other arithmetic: none -> 36.8 us  [from_root(): jnp.sum(lax.all_gather(jnp.where(mine, shard, jnp.zeros_like(shard)), axi...]
  transfers between devices with their start and end apart: 4 -> 7, of which waited for: 3 -> 6; matrix products, arithmetic and copies ran while one was open for 3% -> 5% of each run, Pallas kernels for 0% -> 0%
where the time goes in v1:
time: 1280 us
  waiting for transfers between devices  770 us (60%)
  other arithmetic  176 us (14%)
  blocking collectives  173 us (14%)
  matrix products  77.5 us (6%)
  local copies, waits for them, and re-layouts  67.7 us (5%)
  between operations  17 us (1%)
    all_gather x4, waiting for transfers between devices, from_root(): lax.all_gather(jnp.where(mine, shard, jnp.zeros_like(shard)), axis)  421 us
    psum x1, waiting for transfers between devices, shards(): weight_grad = lax.psum(local_grad * grad_factor, ('rows', 'rep'))  253 us
    all_gather x4, blocking collectives, from_root(): lax.all_gather(jnp.where(mine, shard, jnp.zeros_like(shard)), axis)  173 us
    scatter-add x16, other arithmetic, advance(): return (carry.at[out_block].add(prod), None)  118 us
    reduce_scatter x1, waiting for transfers between devices, shards(): lax.psum_scatter(terms.reshape(sections * nodes_block, width), 'rows', sc...  94.2 us
    reduce_sum x8, other arithmetic, from_root(): jnp.sum(lax.all_gather(jnp.where(mine, shard, jnp.zeros_like(shard)), axi...  36.8 us
    gather x16, local copies, waits for them, and re-layouts, advance(): picked = source[in_block]  36.5 us
    dot_general x8, matrix products, advance(): jnp.einsum('kij,kjf->kif', vals_block, picked, preferred_element_type=jnp...  36.3 us
  transfers between devices with their start and end apart: 7, of which 6 were waited for; matrix products, arithmetic and copies ran while one was open for 5% of the time, Pallas kernels for 0%

profile of v1, /device:TPU:2, one launch (start us, length us, event | category | flops | bytes accessed | tf_op | source)
XLA Modules:
  0.0 1281.8 jit_solution(440973740810585515)
XLA Ops:
  33.0 90.5 %all-gather.15.cloned.1.call-done = bf16[32768,256]{1,0:T(8,128)(2,1)} async-done(((bf16[1024,256]{1,0:T(8,128)(2,1)}), bf16[32768,256]{1,0:T(8,128)(2,1)}) %all-gather.15.cloned.1.call-update) | async-done | bytes 16777232 | tf_op jit(solution)/shard_map/all_gather | solution.py:9
  123.5 9.7 reduce_sum.97
  133.2 109.4 %all-gather.17.cloned.1.call-done = bf16[32768,256]{1,0:T(8,128)(2,1)} async-done(((bf16[1024,256]{1,0:T(8,128)(2,1)}), bf16[32768,256]{1,0:T(8,128)(2,1)}) %all-gather.17.cloned.1.call-update) | async-done | bytes 16777232 | tf_op jit(solution)/shard_map/all_gather | solution.py:9
  251.4 110.5 %all-gather.19.cloned.1.call-done = bf16[32768,256]{1,0:T(8,128)(2,1)} async-done(((bf16[1024,256]{1,0:T(8,128)(2,1)}), bf16[32768,256]{1,0:T(8,128)(2,1)}) %all-gather.19.cloned.1.call-update) | async-done | bytes 16777232 | tf_op jit(solution)/shard_map/all_gather | solution.py:9
  370.6 110.2 %all-gather.13.cloned.1.call-done = bf16[32768,256]{1,0:T(8,128)(2,1)} async-done(((bf16[1024,256]{1,0:T(8,128)(2,1)}), bf16[32768,256]{1,0:T(8,128)(2,1)}) %all-gather.13.cloned.1.call-update) | async-done | bytes 16777232 | tf_op jit(solution)/shard_map/all_gather | solution.py:9
  480.8 9.5 reduce_sum.96
  490.4 26.2 %while.82 = (s32[]{:T(128)}, f32[8,128,256]{2,1,0:T(8,128)S(1)}, s32[2,32]{1,0:T(2,128)S(1)}, pred[2,32]{1,0:T(4,128)(4,1)S(1)}, bf16[2,32,128,128]{3,2,1,0:T(8,...) while((s32[]{:T(128)}, f32[8,128,256]{2,1,0:T(8,128)S(1)}, ...), condition=%wide.region_12.13_spmd, body=%wide.region_10.12_spmd.sunk | while | flops 270533824 | bytes 24122440 | solution.py:40
  516.7 26.2 %while.83 = (s32[]{:T(128)}, f32[8,128,256]{2,1,0:T(8,128)S(1)}, s32[2,32]{1,0:T(2,128)S(1)}, pred[2,32]{1,0:T(4,128)(4,1)S(1)}, bf16[2,32,128,128]{3,2,1,0:T(8,...) while((s32[]{:T(128)}, f32[8,128,256]{2,1,0:T(8,128)S(1)}, ...), condition=%wide.region_16.17_spmd, body=%wide.region_14.16_spmd.sunk | while | flops 270533824 | bytes 24122440 | solution.py:40
  542.9 28.3 %while.80 = (s32[]{:T(128)}, f32[8,128,256]{2,1,0:T(8,128)S(1)}, s32[2,32]{1,0:T(2,128)S(1)}, pred[2,32]{1,0:T(4,128)(4,1)S(1)}, bf16[2,32,128,128]{3,2,1,0:T(8,...) while((s32[]{:T(128)}, f32[8,128,256]{2,1,0:T(8,128)S(1)}, ...), condition=%wide.region_4.5_spmd, body=%wide.region_2.4_spmd.sunk | while | flops 270533824 | bytes 24122440 | solution.py:40
  572.3 34.8 %while.81 = (s32[]{:T(128)}, f32[8,128,256]{2,1,0:T(8,128)}, s32[2,32]{1,0:T(2,128)S(1)}, pred[2,32]{1,0:T(4,128)(4,1)S(1)}, bf16[2,32,128,128]{3,2,1,0:T(8,128)...) while((s32[]{:T(128)}, f32[8,128,256]{2,1,0:T(8,128)}, s32[2,32]{1,0:T(2,128)S(1)}, ...), condition=%wide.region_8.9_spmd, body=%wide.region_6.8_spmd.sunk | while | flops 270533824 | bytes 24122440 | solution.py:40
  579.9 9.8 scatter_fusion.1
  597.3 9.8 scatter_fusion.1
  624.3 53.5 %all-gather.4 = bf16[32768]{0:T(1024)(128)(2,1)S(1)} all-gather(bf16[1024]{0:T(1024)(128)(2,1)S(1)} %copy-done.15), channel_id=6, replica_groups=mesh['rows'=32,'rep'=8] {'rows'}, dimensions={0}, use_global_device_ids=true | all-gather | bytes 67584 | tf_op jit(solution)/shard_map/all_gather | solution.py:9
  677.9 39.3 %all-gather.5 = bf16[32768]{0:T(1024)(128)(2,1)S(1)} all-gather(bf16[1024]{0:T(1024)(128)(2,1)S(1)} %copy-done.14), channel_id=7, replica_groups=mesh['rows'=32,'rep'=8] {'rows'}, dimensions={0}, use_global_device_ids=true | all-gather | bytes 67584 | tf_op jit(solution)/shard_map/all_gather | solution.py:9
  717.3 40.7 %all-gather.7 = bf16[32768]{0:T(1024)(128)(2,1)S(1)} all-gather(bf16[1024]{0:T(1024)(128)(2,1)S(1)} %copy-done.13), channel_id=9, replica_groups=mesh['rows'=32,'rep'=8] {'rows'}, dimensions={0}, use_global_device_ids=true | all-gather | bytes 67584 | tf_op jit(solution)/shard_map/all_gather | solution.py:9
  758.0 39.3 %all-gather.6 = bf16[32768]{0:T(1024)(128)(2,1)S(1)} all-gather(bf16[1024]{0:T(1024)(128)(2,1)S(1)} %copy-done.12), channel_id=8, replica_groups=mesh['rows'=32,'rep'=8] {'rows'}, dimensions={0}, use_global_device_ids=true | all-gather | bytes 67584 | tf_op jit(solution)/shard_map/all_gather | solution.py:9
  802.2 26.2 %while.87 = (s32[]{:T(128)}, f32[8,128,256]{2,1,0:T(8,128)S(1)}, s32[2,32]{1,0:T(2,128)S(1)}, pred[2,32]{1,0:T(4,128)(4,1)S(1)}, bf16[2,32,128,128]{2,3,1,0:T(8,...) while((s32[]{:T(128)}, f32[8,128,256]{2,1,0:T(8,128)S(1)}, ...), condition=%wide.region_30.31_spmd, body=%wide.region_28.30_spmd.sunk | while | flops 270533824 | bytes 24122440 | solution.py:40
  828.5 26.0 %while.86 = (s32[]{:T(128)}, f32[8,128,256]{2,1,0:T(8,128)S(1)}, s32[2,32]{1,0:T(2,128)S(1)}, pred[2,32]{1,0:T(4,128)(4,1)S(1)}, bf16[2,32,128,128]{2,3,1,0:T(8,...) while((s32[]{:T(128)}, f32[8,128,256]{2,1,0:T(8,128)S(1)}, ...), condition=%wide.region_27.28_spmd, body=%wide.region_25.27_spmd.sunk | while | flops 270533824 | bytes 24122440 | solution.py:40
  855.8 34.2 %while.85 = (s32[]{:T(128)}, f32[8,128,256]{2,1,0:T(8,128)}, s32[2,32]{1,0:T(2,128)S(1)}, pred[2,32]{1,0:T(4,128)(4,1)S(1)}, bf16[2,32,128,128]{2,3,1,0:T(8,128)...) while((s32[]{:T(128)}, f32[8,128,256]{2,1,0:T(8,128)}, ...), condition=%wide.region_24.25_spmd, body=%wide.region_22.24_spmd.sunk | while | flops 270533824 | bytes 24122440 | solution.py:40
  862.4 11.1 scatter_fusion.5
  880.2 9.8 scatter_fusion.5
  890.1 26.1 %while.84 = (s32[]{:T(128)}, f32[8,128,256]{2,1,0:T(8,128)S(1)}, s32[2,32]{1,0:T(2,128)S(1)}, pred[2,32]{1,0:T(4,128)(4,1)S(1)}, bf16[2,32,128,128]{2,3,1,0:T(8,...) while((s32[]{:T(128)}, f32[8,128,256]{2,1,0:T(8,128)S(1)}, ...), condition=%wide.region_21.22_spmd, body=%wide.region_19.21_spmd.sunk | while | flops 270533824 | bytes 24122440 | solution.py:40
  924.6 94.2 %reduce-scatter.2.cloned.1.call-done = f32[128,256]{1,0:T(8,128)} async-done(((f32[4096,256]{1,0:T(8,128)}), f32[128,256]{1,0:T(8,128)}) %reduce-scatter.2.cloned.1.call-update) | async-done | bytes 131088 | tf_op jit(solution)/shard_map/reduce_scatter | solution.py:130
  1020.4 252.9 %all-reduce.5.cloned.1.call-done = f32[256,256]{1,0:T(8,128)} async-done(((f32[256,256]{1,0:T(8,128)}), f32[256,256]{1,0:T(8,128)}) %all-reduce.5.cloned.1.call-update) | async-done | bytes 262160 | tf_op jit(solution)/shard_map/psum | solution.py:110
  (203 shorter events, 263.9 us)
Async XLA Ops:
  7.2 791.8 %copy-start = (bf16[256,256]{1,0:T(8,128)(2,1)S(1)}, bf16[256,256]{1,0:T(8,128)(2,1)}, u32[]{:S(2)}) copy-start(bf16[256,256]{1,0:T(8,128)(2,1)} %param.26) | copy-start | bytes 393220
  7.2 116.3 %all-gather.15.cloned.1.call-start = ((), (), s32[]{:S(2)}) async-start(), calls=%async_computation.5 | async-start | bytes 17301504 | tf_op jit(solution)/shard_map/all_gather | solution.py:9
  9.2 4.8 copy-start.17
  9.2 8.2 copy-start.10
  9.2 8.2 copy-start.11
  11.9 230.7 %all-gather.17.cloned.1.call-start = ((), (), s32[]{:S(2)}) async-start(), calls=%async_computation.6 | async-start | bytes 17301504 | tf_op jit(solution)/shard_map/all_gather | solution.py:9
  12.7 349.2 %all-gather.19.cloned.1.call-start = ((), (), s32[]{:S(2)}) async-start(), calls=%async_computation.7 | async-start | bytes 17301504 | tf_op jit(solution)/shard_map/all_gather | solution.py:9
  13.4 467.4 %all-gather.13.cloned.1.call-start = ((), (), s32[]{:S(2)}) async-start(), calls=%async_computation.4 | async-start | bytes 17301504 | tf_op jit(solution)/shard_map/all_gather | solution.py:9
  14.0 783.5 %all-reduce.3.cloned.1.call-start = ((), (), s32[]{:S(2)}) async-start(), calls=%async_computation.1 | async-start | bytes 2097152 | tf_op jit(solution)/shard_map/psum | solution.py:93
  609.6 409.2 %reduce-scatter.2.cloned.1.call-start = ((), (), s32[]{:S(2)}) async-start(), calls=%async_computation.3 | async-start | bytes 4325376 | tf_op jit(solution)/shard_map/reduce_scatter | solution.py:130
  609.7 4.4 copy-start.4
  617.0 4.2 copy-start.3
  621.2 3.1 copy-start.15
  621.2 56.7 %copy-start.14 = (bf16[1024]{0:T(1024)(128)(2,1)S(1)}, bf16[1024]{0:T(1024)(128)(2,1)}, u32[]{:S(2)}) copy-start(bf16[1024]{0:T(1024)(128)(2,1)} %get-tuple-element.566) | copy-start | bytes 6148
  621.2 96.1 %copy-start.13 = (bf16[1024]{0:T(1024)(128)(2,1)S(1)}, bf16[1024]{0:T(1024)(128)(2,1)}, u32[]{:S(2)}) copy-start(bf16[1024]{0:T(1024)(128)(2,1)} %get-tuple-element.568) | copy-start | bytes 6148
  621.2 136.8 %copy-start.12 = (bf16[1024]{0:T(1024)(128)(2,1)S(1)}, bf16[1024]{0:T(1024)(128)(2,1)}, u32[]{:S(2)}) copy-start(bf16[1024]{0:T(1024)(128)(2,1)} %get-tuple-element.569) | copy-start | bytes 6148
  621.3 176.2 %copy-start.6 = (bf16[1024,256]{1,0:T(8,128)(2,1)S(1)}, bf16[1024,256]{1,0:T(8,128)(2,1)}, u32[]{:S(2)}) copy-start(bf16[1024,256]{1,0:T(8,128)(2,1)} %param.24) | copy-start | bytes 1572868
  621.3 176.2 %copy-start.9 = (f32[1024]{0:T(1024)S(1)}, f32[1024]{0:T(1024)}, u32[]{:S(2)}) copy-start(f32[1024]{0:T(1024)} %copy-done.8) | copy-start | bytes 12292
  624.2 174.8 %copy-start.16 = (bf16[1024,256]{1,0:T(8,128)(2,1)S(1)}, bf16[1024,256]{1,0:T(8,128)(2,1)}, u32[]{:S(2)}) copy-start(bf16[1024,256]{1,0:T(8,128)(2,1)} %param.31) | copy-start | bytes 1572868
  799.0 1.8 copy-start.7
  854.5 1.3 copy-start.2
  916.2 2.0 copy-start.5
  921.1 353.8 %copy-start.1 = (bf16[256,256]{1,0:T(8,128)(2,1)S(1)}, bf16[256,256]{1,0:T(8,128)(2,1)}, u32[]{:S(2)}) copy-start(bf16[256,256]{1,0:T(8,128)(2,1)} %param.26) | copy-start | bytes 393220
  921.1 352.1 %all-reduce.5.cloned.1.call-start = ((), (), s32[]{:S(2)}) async-start(), calls=%async_computation.2 | async-start | bytes 524288 | tf_op jit(solution)/shard_map/psum | solution.py:110
  (1 other events, 0.6 us)
Sparse Core Ops, SparseCore 0:
  12.0 111.3 all-gather.14
  126.0 116.5 all-gather.16
  245.2 116.5 all-gather.18
  364.2 116.5 all-gather.12
  609.7 88.0 all-reduce.2
  921.3 97.5 reduce-scatter.1
  1025.7 247.4 all-reduce.4
